TPU v7x, 32 devices: a whole 2x2x4 slice. The times are simulated.
32 devices in a mesh: task: 16 (over z, y, x), shard: 2 (over core).
Axes of the slice: x: 2, y: 2, z: 4, core: 2. Of those that a mesh axis runs over, the one named last changes fastest.
Arguments:
- tokens: bfloat16 [16, 512, 1024], P('task'), may hold values from -6 to 6
- targets: bfloat16 [16, 512, 1024], P('task'), may hold values from -6 to 6
- meta_tokens: bfloat16 [16, 512, 1024], P('task'), may hold values from -6 to 6
- meta_targets: bfloat16 [16, 512, 1024], P('task'), may hold values from -6 to 6
- gate_weight: bfloat16 [16, 1024, 1536], P('task', None, 'shard'), may hold values from -0.1875 to 0.1875
- up_weight: bfloat16 [16, 1024, 1536], P('task', None, 'shard'), may hold values from -0.1875 to 0.1875
- down_weight: bfloat16 [16, 1536, 1024], P('task', 'shard'), may hold values from -0.15625 to 0.15625
- task_step: int32 [16], P('task'), may hold values from 0 to 9999
- hidden_state: float32 [16, 3, 512], P('task'), may hold values from -3 to 3
- cell_state: float32 [16, 3, 512], P('task'), may hold values from -6 to 6
- recurrent_weight: float32 [512, 2048], P('task'), may hold values from -0.25 to 0.25
- input_weight: float32 [3, 2048], replicated, may hold values from -3.5 to 3.5
- lstm_bias: float32 [2048], replicated, may hold values from -3 to 3
- context_weight: float32 [512, 5], replicated, may hold values from -0.25 to 0.25
- mlp_weight: float32 [3, 4], replicated, may hold values from -4 to 4
Outputs:
- gate_update: bfloat16 [16, 1024, 1536], P('task', None, 'shard')
- up_update: bfloat16 [16, 1024, 1536], P('task', None, 'shard')
- down_update: bfloat16 [16, 1536, 1024], P('task', 'shard')
- new_hidden: float32 [16, 3, 512], P('task')
- new_cell: float32 [16, 3, 512], P('task')
- meta_loss: float32 [], replicated
All inputs are finite; a program needn't handle non-finite values.
Results may differ from a plain program's by a relative error of at most 0.0056.
Values sent between devices are 32-bit elements; how exact they have to be, the bound alone decides.
A program may use at most 128 MiB of HBM per device.

v0:
```python
import jax
import jax.numpy as jnp
from jax import lax
from jax.sharding import PartitionSpec as P

STEPS = 10000


highest = lax.Precision.HIGHEST
epsilon = 1e-06
rate_factor = 0.1


def block_forward(inputs, w_gate, w_up, w_down):
    gate_pre = jnp.dot(inputs, w_gate, preferred_element_type=jnp.float32)
    up_pre = jnp.dot(inputs, w_up, preferred_element_type=jnp.float32)
    sigmoid_gate = jax.nn.sigmoid(gate_pre)
    activated = (gate_pre * sigmoid_gate * up_pre).astype(jnp.bfloat16)
    output = jnp.dot(activated, w_down, preferred_element_type=jnp.float32)
    return (gate_pre, up_pre, sigmoid_gate, activated, output)


def block_grads(inputs, w_down, gate_pre, up_pre, sigmoid_gate, activated, d_out):
    d_act = lax.dot_general(
        d_out, w_down, (((1,), (1,)), ((), ())), preferred_element_type=jnp.float32
    )
    d_gate = (d_act * up_pre * sigmoid_gate * (1.0 + gate_pre * (1.0 - sigmoid_gate))).astype(
        jnp.bfloat16
    )
    d_up = (d_act * gate_pre * sigmoid_gate).astype(jnp.bfloat16)
    grad_gate = lax.dot_general(
        inputs, d_gate, (((0,), (0,)), ((), ())), preferred_element_type=jnp.float32
    )
    grad_up = lax.dot_general(
        inputs, d_up, (((0,), (0,)), ((), ())), preferred_element_type=jnp.float32
    )
    grad_down = lax.dot_general(
        activated, d_out, (((0,), (0,)), ((), ())), preferred_element_type=jnp.float32
    )
    return (grad_gate, grad_up, grad_down)


def lstm_step(features, recurrent_term, cell_old, input_weight, lstm_bias, context_weight):
    state_width = cell_old.shape[-1]
    lstm_in = jnp.dot(features, input_weight, precision=highest) + recurrent_term + lstm_bias
    in_gate = jax.nn.sigmoid(lstm_in[:, :state_width])
    forget_gate = jax.nn.sigmoid(lstm_in[:, state_width : 2 * state_width])
    candidate = jnp.tanh(lstm_in[:, 2 * state_width : 3 * state_width])
    out_gate = jax.nn.sigmoid(lstm_in[:, 3 * state_width :])
    cell_new = forget_gate * cell_old + in_gate * candidate
    hidden_new = out_gate * jnp.tanh(cell_new)
    context = jnp.dot(hidden_new, context_weight, precision=highest)
    return (hidden_new, cell_new, context)


def param_update(param, gradient, rms_param, rms_grad, context_row, mlp_weight):
    p_norm = param.astype(jnp.float32) / rms_param
    g_norm = gradient / rms_grad
    summed = jnp.zeros(param.shape, jnp.float32)
    for hidden_unit in range(mlp_weight.shape[1]):
        inner = (
            mlp_weight[0, hidden_unit] * p_norm
            + mlp_weight[1, hidden_unit] * g_norm
            + context_row[hidden_unit]
        )
        summed = summed + mlp_weight[2, hidden_unit] * jax.nn.relu(inner)
    update = jnp.exp(context_row[-1]) * summed
    new_param = (param.astype(jnp.float32) - rate_factor * rms_param * update).astype(jnp.bfloat16)
    return (update.astype(jnp.bfloat16), new_param)


def local(
    tokens,
    targets,
    meta_tokens,
    meta_targets,
    gate_weight,
    up_weight,
    down_weight,
    task_step,
    hidden_state,
    cell_state,
    recurrent_weight,
    input_weight,
    lstm_bias,
    context_weight,
    mlp_weight,
):
    inputs = tokens[0]
    wanted = targets[0]
    meta_in = meta_tokens[0]
    meta_want = meta_targets[0]
    params = (gate_weight[0], up_weight[0], down_weight[0])
    gate_pre, up_pre, sigmoid_gate, activated, partial_out = block_forward(
        inputs, params[0], params[1], params[2]
    )
    output = lax.psum(partial_out, "shard")
    d_out = (output - wanted.astype(jnp.float32)).astype(jnp.bfloat16)
    gradients = block_grads(inputs, params[2], gate_pre, up_pre, sigmoid_gate, activated, d_out)
    grad_sq = jnp.stack([jnp.sum(grad_piece * grad_piece) for grad_piece in gradients])
    param_sq = jnp.stack(
        [jnp.sum(jnp.square(param_piece.astype(jnp.float32))) for param_piece in params]
    )
    tensor_sums = lax.psum(jnp.stack([grad_sq, param_sq]), "shard")
    entries = float(params[0].size * lax.axis_size("shard"))
    rms_grad = jnp.sqrt(tensor_sums[0] / entries + epsilon)
    rms_param = jnp.sqrt(tensor_sums[1] / entries + epsilon)
    fraction = jnp.full((3,), task_step[0].astype(jnp.float32) / STEPS, jnp.float32)
    features = jnp.stack([jnp.log(rms_grad), jnp.log(rms_param), fraction], axis=1)
    hidden_old = hidden_state[0]
    recurrent_term = jnp.dot(
        hidden_old, lax.all_gather(recurrent_weight, "task", axis=0, tiled=True), precision=highest
    )
    hidden_new, cell_new, context = lstm_step(
        features, recurrent_term, cell_state[0], input_weight, lstm_bias, context_weight
    )
    results = [
        param_update(
            params[tensor_id],
            gradients[tensor_id],
            rms_param[tensor_id],
            rms_grad[tensor_id],
            context[tensor_id],
            mlp_weight,
        )
        for tensor_id in range(3)
    ]
    meta_partial = block_forward(meta_in, results[0][1], results[1][1], results[2][1])[4]
    loss_scale = 0.5 / (meta_want.shape[0] * meta_want.shape[1])
    meta_share = lax.psum_scatter(meta_partial, "shard", scatter_dimension=1, tiled=True)
    share_cols = meta_share.shape[1]
    want_share = lax.dynamic_slice_in_dim(
        meta_want, lax.axis_index("shard") * share_cols, share_cols, 1
    )
    meta_part = loss_scale * jnp.sum(jnp.square(meta_share - want_share.astype(jnp.float32)))
    summed = lax.psum(meta_part, ("task", "shard"))
    meta_loss = summed / lax.axis_size("task")
    return (
        results[0][0][None],
        results[1][0][None],
        results[2][0][None],
        hidden_new[None],
        cell_new[None],
        meta_loss,
    )


def solution(mesh):
    return jax.shard_map(
        local,
        mesh=mesh,
        in_specs=(
            P("task", None, None),
            P("task", None, None),
            P("task", None, None),
            P("task", None, None),
            P("task", None, "shard"),
            P("task", None, "shard"),
            P("task", "shard", None),
            P("task"),
            P("task", None, None),
            P("task", None, None),
            P("task", None),
            P(),
            P(),
            P(),
            P(),
        ),
        out_specs=(
            P("task", None, "shard"),
            P("task", None, "shard"),
            P("task", "shard", None),
            P("task", None, None),
            P("task", None, None),
            P(),
        ),
        check_vma=False,
    )
```

profile of v0, /device:TPU:0, one launch (start us, length us, event | category | flops | bytes accessed | tf_op | source)
XLA Modules:
  0.0 225.3 jit_solution(7514482021820399542)
XLA Ops:
  9.2 2.4 %fusion.48 = f32[512,768]{1,0:T(8,128)S(1)} fusion(bf16[1,1024,768]{2,1,0:T(8,128)(2,1)} %param.19, bf16[1,512,1024]{2,1,0:T(8,128)(2,1)S(1)} %copy-done), kind=kOutput, calls=%fused_computation.68 | convolution fusion | flops 805306368 | bytes 4194304 | tf_op jit(solution)/shard_map/dot_general | solution.py:15
  11.7 2.1 multiply_convert_fusion.2
  13.8 2.3 %fusion.57 = f32[512,1024]{1,0:T(8,128)} fusion(bf16[512,768]{1,0:T(8,128)(2,1)S(1)} %get-tuple-element.57, bf16[1,768,1024]{2,1,0:T(8,128)(2,1)S(1)} %copy-done.4), kind=kOutput, calls=%fused_computation.80 | convolution fusion | flops 805306368 | bytes 4456448 | tf_op jit(solution)/shard_map/dot_general | solution.py:19
  16.8 1.7 copy.22
  18.5 2.6 %copy.21 = bf16[1,1024,768]{1,2,0:T(8,128)(2,1)} copy(bf16[1,1024,768]{2,1,0:T(8,128)(2,1)} %param.19) | data formatting | bytes 3145728 | tf_op args[4]
  22.6 2.8 %fusion.4 = f32[]{:T(128)} fusion(bf16[1,768,1024]{2,1,0:T(8,128)(2,1)} %param.21), kind=kLoop, calls=%fused_computation.13 | loop fusion | flops 2359295 | bytes 1572868 | tf_op jit(solution)/shard_map/reduce_sum | solution.py:102
  28.3 12.0 %all-reduce.2.cloned.1.call-done = f32[512,1024]{1,0:T(8,128)} async-done(((f32[512,1024]{1,0:T(8,128)}), f32[512,1024]{1,0:T(8,128)}) %all-reduce.2.cloned.1.call-update) | async-done | bytes 2097168 | tf_op jit(solution)/shard_map/psum | solution.py:97
  40.3 3.5 %fusion.55 = f32[512,768]{1,0:T(8,128)S(1)} fusion(bf16[1,768,1024]{2,1,0:T(8,128)(2,1)} %param.21, f32[512,1024]{1,0:T(8,128)} %all-reduce.2.cloned.1.call-done, bf16[1,512,1024]{2,1,0:T(8,128)(2,1)} %param.16), kind=kOutput, calls=%fused_computation.78 | convolution fusion | flops 806879232 | bytes 6291456 | tf_op jit(solution)/shard_map/dot_general | solution.py:24
  43.9 3.3 %multiply_reduce_fusion = (f32[]{:T(128)}, f32[768,1024]{1,0:T(8,128)}) fusion(bf16[512,768]{1,0:T(8,128)(2,1)S(1)} %get-tuple-element.57, f32[512,1024]{1,0:T(8,128)S(1)} %copy-done.6, bf16[1,512,1024]{2,1,0:T(8,128)(2,1)S(1)} %copy-done.8), kind=kOutput, calls=%fused_computation.56 | convolution fusion | flops 808452096 | bytes 7077892 | tf_op jit(solution)/shard_map/dot_general | solution.py:37
  47.3 3.5 %multiply_reduce_fusion.1 = (f32[]{:T(128)}, f32[768,1024]{1,0:T(8,128)}) fusion(bf16[1,512,1024]{2,1,0:T(8,128)(2,1)S(1)} %copy-done, f32[512,768]{1,0:T(8,128)S(1)} %fusion.55, f32[512,768]{1,0:T(8,128)S(1)} %copy-done.21), kind=kOutput, calls=%fused_computation.57 | convolution fusion | flops 809238528 | bytes 7340036 | tf_op jit(solution)/shard_map/dot_general | solution.py:34
  50.7 3.6 %multiply_reduce_fusion.2 = (f32[]{:T(128)}, f32[768,1024]{1,0:T(8,128)}) fusion(bf16[1,512,1024]{2,1,0:T(8,128)(2,1)S(1)} %copy-done, f32[512,768]{1,0:T(8,128)S(1)} %copy-done.21, f32[512,768]{1,0:T(8,128)S(1)} %fusion.55, f32[512,768]{1,0:T(8,128)S(1)} %copy-done.22), kind=kOutput, calls=%fused_computation.58 | convolution fusion | flops 810811392 | bytes 8912900 | tf_op jit(solution)/shard_map/dot_general | solution.py:31
  54.3 3.9 %maximum_bitcast_fusion = (f32[1,3]{1,0:T(1,128)S(1)}, f32[1,3]{1,0:T(1,128)S(1)}) fusion(f32[1]{0:T(128)} %bitcast.7, f32[1]{0:T(128)} %bitcast.6, f32[1]{0:T(128)} %bitcast.5, f32[1]{0:T(128)} %bitcast.11, f32[1]{0:T(128)} %bitcast.10, f32[1]{0:T(128)} %bitcast.9), kind=kLoop, calls=%fused_computation.130 | loop fusion | flops 12 | bytes 48 | tf_op jit(solution)/shard_map/stack | solution.py:104
  58.3 2.6 %psum.22 = f32[2,3]{1,0:T(2,128)S(1)} all-reduce(f32[2,3]{1,0:T(2,128)S(1)} %pad_maximum_fusion), channel_id=1, replica_groups=mesh['task'=16,'shard'=2] {'shard'}, use_global_device_ids=true, to_apply=%region_7.0 | all-reduce | flops 6 | bytes 48 | tf_op jit(solution)/shard_map/psum | solution.py:104
  64.3 33.4 %all-gather.2.cloned.1.call-done = f32[512,2048]{1,0:T(8,128)} async-done(((f32[32,2048]{1,0:T(8,128)}), f32[512,2048]{1,0:T(8,128)}) %all-gather.2.cloned.1.call-update) | async-done | bytes 4194320 | tf_op jit(solution)/shard_map/all_gather | solution.py:112
  97.7 4.4 %fusion.38 = f32[3,2048]{1,0:T(4,128)S(1)} fusion(f32[3,2048]{1,0:T(4,128)S(1)} %fusion.93, f32[512,2048]{1,0:T(8,128)} %all-gather.2.cloned.1.call-done, f32[2048]{0:T(1024)S(1)} %copy-done.18, f32[1,3,512]{2,0,1:T(1,128)S(1)} %copy-done.17), kind=kOutput, calls=%fused_computation.60 | convolution fusion | flops 37761024 | bytes 4257792 | tf_op jit(solution)/shard_map/dot_general | solution.py:111
  105.0 15.6 %convert_bitcast_fusion.1 = (bf16[1,1024,768]{1,2,0:T(8,128)(2,1)}, f32[1024,768]{0,1:T(8,128)S(1)}) fusion(f32[]{:T(128)} %bitcast.50, f32[]{:T(128)} %bitcast.36, f32[]{:T(128)} %bitcast.35, f32[]{:T(128)} %bitcast.34, f32[]{:T(128)} %bitcast.48, f32[]{:T(128)} %bitcast.31, f32[]{:T(128)} %bitcast.30, f32[]{:T(128)} %bitcast.29, f32[]{:T(128)} %bitcast.46, ...), kind=kLoop, calls=%fused_computation.88 | loop fusion | flops 25165824 | bytes 9437260 | tf_op jit(solution)/shard_map/broadcast_in_dim | solution.py:140
  120.6 2.3 %fusion.42 = f32[768,512]{0,1:T(8,128)} fusion(f32[1024,768]{0,1:T(8,128)S(1)} %get-tuple-element.15, bf16[1,1024,768]{1,2,0:T(8,128)(2,1)S(1)} %copy.22, f32[]{:T(128)S(6)} %mul.394, bf16[1,512,1024]{2,1,0:T(8,128)(2,1)S(1)} %copy-done.12), kind=kOutput, calls=%fused_computation.64 | convolution fusion | flops 808452096 | bytes 7340036 | tf_op jit(solution)/shard_map/dot_general | solution.py:16
  123.5 16.5 %convert_bitcast_fusion = (bf16[1,768,1024]{2,1,0:T(8,128)(2,1)}, f32[768,1024]{1,0:T(8,128)}) fusion(f32[]{:T(128)} %bitcast.58, f32[]{:T(128)} %bitcast.36, f32[]{:T(128)} %bitcast.35, f32[]{:T(128)} %bitcast.34, f32[]{:T(128)} %bitcast.57, f32[]{:T(128)} %bitcast.31, f32[]{:T(128)} %bitcast.30, f32[]{:T(128)} %bitcast.29, f32[]{:T(128)} %bitcast.56, ...), kind=kLoop, calls=%fused_computation.87 | loop fusion | flops 25165824 | bytes 9437260 | tf_op jit(solution)/shard_map/broadcast_in_dim | solution.py:141
  140.1 16.0 %convert_bitcast_fusion.2 = (bf16[1,1024,768]{1,2,0:T(8,128)(2,1)}, f32[1024,768]{0,1:T(8,128)}) fusion(f32[]{:T(128)} %bitcast.38, f32[]{:T(128)} %bitcast.36, f32[]{:T(128)} %bitcast.35, f32[]{:T(128)} %bitcast.34, f32[]{:T(128)} %bitcast.33, f32[]{:T(128)} %bitcast.31, f32[]{:T(128)} %bitcast.30, f32[]{:T(128)} %bitcast.29, f32[]{:T(128)} %bitcast.28, ...), kind=kLoop, calls=%fused_computation.89 | loop fusion | flops 25165824 | bytes 9437260 | tf_op jit(solution)/shard_map/broadcast_in_dim | solution.py:139
  156.1 7.8 %fusion.40 = f32[512,1024]{1,0:T(8,128)} fusion(f32[768,1024]{1,0:T(8,128)} %get-tuple-element.13, bf16[1,768,1024]{2,1,0:T(8,128)(2,1)} %param.21, f32[]{:T(128)S(6)} %mul.398, f32[768,512]{0,1:T(8,128)} %fusion.42, bf16[1,512,1024]{2,1,0:T(8,128)(2,1)} %param.17, f32[1024,768]{0,1:T(8,128)} %get-tuple-element.17, bf16[1,1024,768]{1,2,0:T(8,128)(2,1)S(1)} %copy-done.3, ...), kind=kOutput, calls=%fused_computation.63 | convolution fusion | flops 1619263488 | bytes 14155784 | tf_op jit(solution)/shard_map/dot_general | solution.py:19
  166.8 2.7 %copy.24 = bf16[1,1024,768]{2,1,0:T(8,128)(2,1)} copy(bf16[1,1024,768]{1,2,0:T(8,128)(2,1)} %get-tuple-element.16) | data formatting | bytes 3145728
  170.1 2.2 reduce-scatter.2.cloned.1.call-done
  172.3 2.1 fusion.65
  175.6 40.5 %psum.23 = f32[]{:T(128)} all-reduce(f32[]{:T(128)S(6)} %mul_shard_map.3), channel_id=1, replica_groups=mesh['task'=16,'shard'=2] {'task','shard'}, use_global_device_ids=true, to_apply=%region_10.11 | all-reduce | flops 1 | bytes 8 | tf_op jit(solution)/shard_map/psum | solution.py:136
  (67 shorter events, 12.9 us)
Async XLA Ops:
  8.0 3.6 %copy-start.11 = (bf16[1,1024,768]{2,1,0:T(8,128)(2,1)S(1)}, bf16[1,1024,768]{2,1,0:T(8,128)(2,1)}, u32[]{:S(2)}) copy-start(bf16[1,1024,768]{2,1,0:T(8,128)(2,1)} %param.20) | copy-start | bytes 4718596
  8.0 32.3 %all-reduce.2.cloned.1.call-start = ((), (), s32[]{:S(2)}) async-start(), calls=%async_computation.1 | async-start | bytes 4194304 | tf_op jit(solution)/shard_map/psum | solution.py:97
  11.6 2.2 copy-start.20
  11.6 2.2 copy-start.4
  16.2 81.5 %all-gather.2.cloned.1.call-start = ((), (), s32[]{:S(2)}) async-start(), calls=%async_computation.2 | async-start | bytes 4456448 | tf_op jit(solution)/shard_map/all_gather | solution.py:112
  16.7 5.1 %copy-start.15 = (f32[3,4]{1,0:T(4,128)S(1)}, f32[3,4]{1,0:T(4,128)}, u32[]{:S(2)}) copy-start(f32[3,4]{1,0:T(4,128)} %param.29) | copy-start | bytes 148
  16.8 155.5 %reduce-scatter.2.cloned.1.call-start = ((), (), s32[]{:S(2)}) async-start(), calls=%async_computation.3 | async-start | bytes 3145728 | tf_op jit(solution)/shard_map/reduce_scatter | solution.py:130
  21.1 5.7 %copy-start.2 = (bf16[1,1024,768]{1,2,0:T(8,128)(2,1)S(1)}, bf16[1,1024,768]{1,2,0:T(8,128)(2,1)}, u32[]{:S(2)}) copy-start(bf16[1,1024,768]{1,2,0:T(8,128)(2,1)} %copy.21) | copy-start | bytes 4718596
  40.3 3.5 %copy-start.6 = (f32[512,1024]{1,0:T(8,128)S(1)}, f32[512,1024]{1,0:T(8,128)}, u32[]{:S(2)}) copy-start(f32[512,1024]{1,0:T(8,128)} %all-reduce.2.cloned.1.call-done) | copy-start | bytes 6291460
  40.3 3.5 %copy-start.8 = (bf16[1,512,1024]{2,1,0:T(8,128)(2,1)S(1)}, bf16[1,512,1024]{2,1,0:T(8,128)(2,1)}, u32[]{:S(2)}) copy-start(bf16[1,512,1024]{2,1,0:T(8,128)(2,1)} %param.16) | copy-start | bytes 3145732
  43.9 3.4 %copy-start.21 = (f32[512,768]{1,0:T(8,128)S(1)}, f32[512,768]{1,0:T(8,128)}, u32[]{:S(2)}) copy-start(f32[512,768]{1,0:T(8,128)} %copy-done.20) | copy-start | bytes 4718596
  47.3 3.5 %copy-start.22 = (f32[512,768]{1,0:T(8,128)S(1)}, f32[512,768]{1,0:T(8,128)}, u32[]{:S(2)}) copy-start(f32[512,768]{1,0:T(8,128)} %get-tuple-element.58) | copy-start | bytes 4718596
  50.7 13.3 %copy-start.14 = (f32[3,2048]{1,0:T(4,128)S(1)}, f32[3,2048]{1,0:T(4,128)}, u32[]{:S(2)}) copy-start(f32[3,2048]{1,0:T(4,128)} %param.26) | copy-start | bytes 73732
  50.7 46.9 %copy-start.17 = (f32[1,3,512]{2,0,1:T(1,128)S(1)}, f32[1,3,512]{2,0,1:T(1,128)}, u32[]{:S(2)}) copy-start(f32[1,3,512]{2,0,1:T(1,128)} %param.23) | copy-start | bytes 18436
  50.7 46.9 %copy-start.18 = (f32[2048]{0:T(1024)S(1)}, f32[2048]{0:T(1024)}, u32[]{:S(2)}) copy-start(f32[2048]{0:T(1024)} %param.27) | copy-start | bytes 24580
  54.3 47.7 %copy-start.19 = (f32[1,3,512]{2,0,1:T(1,128)S(1)}, f32[1,3,512]{2,0,1:T(1,128)}, u32[]{:S(2)}) copy-start(f32[1,3,512]{2,0,1:T(1,128)} %param.24) | copy-start | bytes 18436
  54.3 47.8 %copy-start.16 = (f32[512,5]{0,1:T(8,128)S(1)}, f32[512,5]{0,1:T(8,128)}, u32[]{:S(2)}) copy-start(f32[512,5]{0,1:T(8,128)} %param.28) | copy-start | bytes 30724
  97.7 7.3 %copy-start.10 = (f32[768,1024]{1,0:T(8,128)S(1)}, f32[768,1024]{1,0:T(8,128)}, u32[]{:S(2)}) copy-start(f32[768,1024]{1,0:T(8,128)} %get-tuple-element.62) | copy-start | bytes 9437188
  105.0 15.6 %copy-start.12 = (bf16[1,512,1024]{2,1,0:T(8,128)(2,1)S(1)}, bf16[1,512,1024]{2,1,0:T(8,128)(2,1)}, u32[]{:S(2)}) copy-start(bf16[1,512,1024]{2,1,0:T(8,128)(2,1)} %param.17) | copy-start | bytes 3145732
  120.6 2.3 %copy-start.1 = (f32[768,1024]{1,0:T(8,128)S(1)}, f32[768,1024]{1,0:T(8,128)}, u32[]{:S(2)}) copy-start(f32[768,1024]{1,0:T(8,128)} %get-tuple-element.60) | copy-start | bytes 9437188
  120.6 2.9 %copy-start.5 = (bf16[1,768,1024]{2,1,0:T(8,128)(2,1)S(1)}, bf16[1,768,1024]{2,1,0:T(8,128)(2,1)}, u32[]{:S(2)}) copy-start(bf16[1,768,1024]{2,1,0:T(8,128)(2,1)} %param.21) | copy-start | bytes 4718596
  123.5 16.6 %copy-start.3 = (bf16[1,1024,768]{1,2,0:T(8,128)(2,1)S(1)}, bf16[1,1024,768]{1,2,0:T(8,128)(2,1)}, u32[]{:S(2)}) copy-start(bf16[1,1024,768]{1,2,0:T(8,128)(2,1)} %copy.21) | copy-start | bytes 4718596
  123.5 16.6 %copy-start.9 = (f32[768,1024]{1,0:T(8,128)S(1)}, f32[768,1024]{1,0:T(8,128)}, u32[]{:S(2)}) copy-start(f32[768,1024]{1,0:T(8,128)} %get-tuple-element.64) | copy-start | bytes 9437188
  166.8 5.4 %copy-start.13 = (bf16[1,512,1024]{2,1,0:T(8,128)(2,1)S(1)}, bf16[1,512,1024]{2,1,0:T(8,128)(2,1)}, u32[]{:S(2)}) copy-start(bf16[1,512,1024]{2,1,0:T(8,128)(2,1)} %param.18) | copy-start | bytes 3145732
  (2 other events, 2.6 us)
Sparse Core Ops, SparseCore 0:
  16.3 24.0 all-reduce.1
  164.0 8.2 reduce-scatter.1
Sparse Core Ops, SparseCore 1:
  19.4 78.2 all-gather.1
where the time goes:
time: 226 us; the launch traced here: 225 us
  other arithmetic  59.9 us (27%)
  waiting for transfers between devices  48.1 us (21%)
  blocking collectives  43.1 us (19%)
  matrix products  35.7 us (16%)
  between operations  22.6 us (10%)
  local copies, waits for them, and re-layouts  15.8 us (7%)
    psum x1, blocking collectives, local(): summed = lax.psum(meta_part, ('task', 'shard'))  40.5 us
    all_gather x1, waiting for transfers between devices, local(): lax.all_gather(recurrent_weight, 'task', axis=0, tiled=True)  33.4 us
    broadcast_in_dim x1, other arithmetic, local(): results[2][0][None]  16.5 us
    broadcast_in_dim x1, other arithmetic, local(): results[0][0][None]  16 us
    broadcast_in_dim x1, other arithmetic, local(): results[1][0][None]  15.6 us
    unnamed x52, local copies, waits for them, and re-layouts  13 us
    psum x1, waiting for transfers between devices, local(): output = lax.psum(partial_out, 'shard')  12 us
    dot_general x2, matrix products, block_forward(): output = jnp.dot(activated, w_down, preferred_element_type=jnp.float32)  10.1 us
  transfers between devices with their start and end apart: 3, of which 3 were waited for; matrix products, arithmetic and copies ran while one was open for 16% of the time, Pallas kernels for 0%

commit v1 on v0

v1 whole, which is shorter than its diff:
```python
import functools

import jax
import jax.numpy as jnp
from jax import lax
from jax.experimental import pallas as pl
from jax.experimental.pallas import tpu as pltpu
from jax.sharding import PartitionSpec as P

STEPS = 10000

highest = lax.Precision.HIGHEST
epsilon = 1e-06
rate_factor = 0.1
f32 = jnp.float32
bf16 = jnp.bfloat16
MESH = pl.DeviceIdType.MESH


def dot(a, b, dims=((1,), (0,)), precision=None):
    return lax.dot_general(a, b, (dims, ((), ())), preferred_element_type=f32, precision=precision)


def fold_sq(x):
    x = x * x
    return jnp.sum(x.reshape(x.shape[0] // 8, 8, x.shape[1]), axis=0)


def total(x):
    return jnp.sum(jnp.sum(x, axis=1, keepdims=True), axis=0, keepdims=True)


def kernel(
    n,
    tok_hbm, tgt_hbm, mtok_hbm, mtgt_hbm, gate_hbm, up_hbm, down_hbm,
    step_ref, hid_ref, cell_ref, rw_ref, iw_ref, bias_ref, cw_ref, mlp_ref,
    gu_hbm, uu_hbm, du_hbm, nh_ref, nc_ref, loss_ref,
    tok, tgt, mtok, mtgt, gate, up, down,
    fa, fb, act, part, recv, tok_t, act_t, dout, dgate, dup,
    gg, gu, gd, ug, uu, ud, msend, mown, mrecv,
    hid_pad, hid_all, rec_part, rec_recv, rec_half, rec_full, sq, stat, stat_recv, cell_pad,
    lossv, loss_recv, loss_chip, loss_all,
    in_sem, out_sem, hid_s, hid_r, rec_s, rec_r, loss_s, loss_r, sib_s, sib_r,
):
    me = lax.axis_index("task")
    core = lax.axis_index("shard")
    sib = 1 - core
    toks, width = tok.shape
    ff = gate.shape[1]
    h = hid_pad.shape[1]
    r = rw_ref.shape[0]
    tb = toks // 2
    fbk = 256
    half = rec_half.shape[1]

    barrier = pltpu.get_barrier_semaphore()

    def peer(off):
        return lax.rem(me + off, n)

    @pl.loop(1, n)
    def _(off):
        pl.semaphore_signal(barrier, inc=1, device_id=(peer(off), core), device_id_type=MESH)

    pl.semaphore_signal(barrier, inc=1, device_id=(me, sib), device_id_type=MESH)

    ins = [
        pltpu.make_async_copy(src.at[0], dst, in_sem.at[i])
        for i, (src, dst) in enumerate(
            ((tok_hbm, tok), (gate_hbm, gate), (up_hbm, up), (down_hbm, down), (tgt_hbm, tgt), (mtok_hbm, mtok), (mtgt_hbm, mtgt))
        )
    ]
    for c in ins:
        c.start()

    hid_pad[...] = jnp.zeros_like(hid_pad)
    hid_pad[0:3, :] = hid_ref[0]
    cell_pad[...] = jnp.zeros_like(cell_pad)
    cell_pad[0:3, :] = cell_ref[0]
    sq[...] = jnp.zeros_like(sq)
    hid_all[me] = hid_pad[...]

    def to_task(src, dst, ss, rs, who, slot):
        return pltpu.make_async_remote_copy(
            src_ref=src, dst_ref=dst.at[slot], send_sem=ss.at[who], recv_sem=rs.at[slot],
            device_id=(who, core), device_id_type=MESH,
        )

    def to_sib(src, dst, i):
        return pltpu.make_async_remote_copy(
            src_ref=src, dst_ref=dst, send_sem=sib_s.at[i], recv_sem=sib_r.at[i],
            device_id=(me, sib), device_id_type=MESH,
        )

    pl.semaphore_wait(barrier, n)

    @pl.loop(1, n)
    def _(off):
        to_task(hid_pad, hid_all, hid_s, hid_r, peer(off), me).start()

    ins[0].wait()
    ins[1].wait()
    ins[2].wait()

    def hidden(x, w1, w2, keep):
        @pl.loop(0, ff // fbk)
        def _(j):
            fs = pl.ds(pl.multiple_of(j * fbk, fbk), fbk)
            for i in range(2):
                ts = pl.ds(i * tb, tb)
                g = dot(x[ts, :], w1[:, fs])
                u = dot(x[ts, :], w2[:, fs])
                s = jax.nn.sigmoid(g)
                a = g * s
                act[ts, fs] = (a * u).astype(bf16)
                if keep:
                    fa[ts, fs] = a
                    fb[ts, fs] = u * s * (1.0 + g * (1.0 - s))

    hidden(tok, gate, up, True)
    ins[3].wait()
    for i in range(2):
        part[i] = dot(act[pl.ds(i * tb, tb), :], down[...])
        to_sib(part.at[i], recv.at[i], i).start()

    @pl.loop(1, n)
    def _(off):
        s = peer(off)
        to_task(hid_pad, hid_all, hid_s, hid_r, s, s).wait_recv()

    picks = lax.broadcasted_iota(jnp.int32, (h, r), 0) == lax.broadcasted_iota(jnp.int32, (h, r), 1) + me * r
    mine = dot(hid_all[...].reshape(n * 8, h), picks.astype(f32), precision=highest)
    cols = pl.ds(pl.multiple_of(core * half, half), half)
    rec_part[...] = dot(mine, rw_ref[:, cols], precision=highest).reshape(n, 8, half)

    @pl.loop(1, n)
    def _(off):
        s = peer(off)
        to_task(rec_part.at[s], rec_recv, rec_s, rec_r, s, me).start()

    rec_recv[me] = rec_part[me]

    tok_t[...] = tok[...].T
    act_t[...] = act[...].T

    def param_sq(w, slot):
        @pl.loop(0, w.shape[0] // 64)
        def _(k):
            x = w[pl.ds(pl.multiple_of(k * 64, 64), 64), :].astype(f32)
            x = fold_sq(x)
            sq[slot] += sum(x[:, q * fbk:(q + 1) * fbk] for q in range(x.shape[1] // fbk))

    param_sq(gate, 3)
    param_sq(up, 4)
    param_sq(down, 5)

    ins[4].wait()
    for i in range(2):
        to_sib(part.at[i], recv.at[i], i).wait()
        ts = pl.ds(i * tb, tb)

        @pl.loop(0, tb // 16)
        def _(k):
            rows = pl.ds(pl.multiple_of(k * 16, 16), 16)
            whole = pl.ds(pl.multiple_of(i * tb + k * 16, 16), 16)
            dout[whole, :] = (part[i, rows, :] + recv[i, rows, :] - tgt[whole, :].astype(f32)).astype(bf16)

        @pl.loop(0, ff // fbk)
        def _(j):
            fs = pl.ds(pl.multiple_of(j * fbk, fbk), fbk)
            d_act = dot(dout[ts, :], down[fs, :], ((1,), (1,)))
            dgate[ts, fs] = (d_act * fb[ts, fs]).astype(bf16)
            dup[ts, fs] = (d_act * fa[ts, fs]).astype(bf16)

    def grad(lhs, rhs, out, slot):
        @pl.loop(0, rhs.shape[1] // fbk)
        def _(j):
            fs = pl.ds(pl.multiple_of(j * fbk, fbk), fbk)
            for q in range(lhs.shape[0] // 256):
                rows = pl.ds(q * 256, 256)
                g = dot(lhs[rows, :], rhs[:, fs])
                out[rows, fs] = g
                sq[slot] += fold_sq(g)

    grad(tok_t, dgate, gg, 0)
    grad(tok_t, dup, gu, 1)
    grad(act_t, dout, gd, 2)

    stat[...] = jnp.zeros_like(stat)
    for i in range(6):
        stat[i // 3, i % 3:i % 3 + 1, :] = jnp.broadcast_to(total(sq[i]), (1, 128))
    to_sib(stat, stat_recv, 2).start()

    @pl.loop(1, n)
    def _(off):
        s = peer(off)
        to_task(rec_part.at[s], rec_recv, rec_s, rec_r, s, s).wait_recv()

    rec_half[...] = jnp.sum(rec_recv[...], axis=0)
    to_sib(rec_half, rec_full.at[core], 3).start()
    rec_full[core] = rec_half[...]

    to_sib(stat, stat_recv, 2).wait()
    entries = 2.0 * (width * ff)
    rms = jnp.sqrt((stat[...] + stat_recv[...]) / entries + epsilon)
    rms_g, rms_p = rms[0], rms[1]
    lg, lp = jnp.log(rms_g)[:, 0:1], jnp.log(rms_p)[:, 0:1]
    frac = step_ref[0].astype(f32) / STEPS
    pltpu.make_async_remote_copy(
        src_ref=rec_half, dst_ref=rec_full.at[sib], send_sem=sib_s.at[3], recv_sem=sib_r.at[3],
        device_id=(me, sib), device_id_type=MESH,
    ).wait()

    def block(q):
        qs = pl.ds(q * h, h)
        rec = rec_full[(q * h) // half, :, pl.ds((q * h) % half, h)]
        return lg * iw_ref[0:1, qs] + lp * iw_ref[1:2, qs] + frac * iw_ref[2:3, qs] + rec + bias_ref[0:1, qs]

    cell = jax.nn.sigmoid(block(1)) * cell_pad[...] + jax.nn.sigmoid(block(0)) * jnp.tanh(block(2))
    hid = jax.nn.sigmoid(block(3)) * jnp.tanh(cell)
    nc_ref[0] = cell[0:3]
    nh_ref[0] = hid[0:3]
    ctx = dot(hid, cw_ref[...], precision=highest)

    units = mlp_ref.shape[1]

    def update(t, w, g, out, out_hbm):
        rp, rg = rms_p[t:t + 1, 0:1], rms_g[t:t + 1, 0:1]
        ca = [mlp_ref[0, k] / rp for k in range(units)]
        cb = [mlp_ref[1, k] / rg for k in range(units)]
        cc = [ctx[t:t + 1, k:k + 1] for k in range(units)]
        size = jnp.exp(ctx[t:t + 1, units:units + 1])
        back = rate_factor * rp

        @pl.loop(0, w.shape[0] // 16)
        def _(i):
            rows = pl.ds(pl.multiple_of(i * 16, 16), 16)
            p = w[rows, :].astype(f32)
            gv = g[rows, :]
            acc = None
            for k in range(units):
                term = mlp_ref[2, k] * jnp.maximum(ca[k] * p + cb[k] * gv + cc[k], 0.0)
                acc = term if acc is None else acc + term
            upd = size * acc
            out[rows, :] = upd.astype(bf16)
            w[rows, :] = (p - back * upd).astype(bf16)

        return pltpu.make_async_copy(out, out_hbm.at[0], out_sem.at[t])

    outs = []
    for t, (w, g, o, oh) in enumerate(((gate, gg, ug, gu_hbm), (up, gu, uu, uu_hbm), (down, gd, ud, du_hbm))):
        c = update(t, w, g, o, oh)
        c.start()
        outs.append(c)

    ins[5].wait()
    hidden(mtok, gate, up, False)
    msend[...] = dot(act[pl.ds(pl.multiple_of(sib * tb, tb), tb), :], down[...])
    to_sib(msend, mrecv, 4).start()
    own = pl.multiple_of(core * tb, tb)
    mown[...] = dot(act[pl.ds(own, tb), :], down[...])
    ins[6].wait()
    to_sib(msend, mrecv, 4).wait()
    lossv[...] = jnp.zeros_like(lossv)

    @pl.loop(0, tb // 16)
    def _(k):
        rows = pl.ds(pl.multiple_of(k * 16, 16), 16)
        d = mown[rows, :] + mrecv[rows, :] - mtgt[pl.ds(pl.multiple_of(own + k * 16, 16), 16), :].astype(f32)
        d = fold_sq(d)
        lossv[...] += sum(d[:, q * 128:(q + 1) * 128] for q in range(width // 128))

    to_sib(lossv, loss_recv, 5).start()
    to_sib(lossv, loss_recv, 5).wait()
    chip = lossv[...] + loss_recv[...]
    loss_chip[...] = chip
    loss_all[me] = chip

    @pl.loop(1, n)
    def _(off):
        to_task(loss_chip, loss_all, loss_s, loss_r, peer(off), me).start()

    for c in outs:
        c.wait()

    @pl.loop(1, n)
    def _(off):
        s = peer(off)
        to_task(hid_pad, hid_all, hid_s, hid_r, s, me).wait_send()
        to_task(rec_part.at[s], rec_recv, rec_s, rec_r, s, me).wait_send()
        to_task(loss_chip, loss_all, loss_s, loss_r, s, me).wait_send()
        to_task(loss_chip, loss_all, loss_s, loss_r, s, s).wait_recv()

    loss_ref[0, 0] = jnp.sum(jnp.sum(loss_all[...], axis=0)) * (0.5 / (toks * width)) / n


def local(*args):
    n = lax.axis_size("task")
    (tokens, targets, mtokens, mtargets, gate, up, down, step, hid, cell, rw, iw, bias, cw, mlp) = args
    toks, width = tokens.shape[1:]
    ff = gate.shape[2]
    h = hid.shape[2]
    r = rw.shape[0]
    half = rw.shape[1] // 2
    vm = pl.BlockSpec(memory_space=pltpu.VMEM)
    sm = pl.BlockSpec(memory_space=pltpu.SMEM)
    anys = pl.BlockSpec(memory_space=pl.ANY)
    V = pltpu.VMEM
    dma = pltpu.SemaphoreType.DMA
    tb = toks // 2
    outs = pl.pallas_call(
        functools.partial(kernel, n),
        out_shape=(
            jax.ShapeDtypeStruct(gate.shape, bf16),
            jax.ShapeDtypeStruct(up.shape, bf16),
            jax.ShapeDtypeStruct(down.shape, bf16),
            jax.ShapeDtypeStruct(hid.shape, f32),
            jax.ShapeDtypeStruct(cell.shape, f32),
            jax.ShapeDtypeStruct((1, 1), f32),
        ),
        in_specs=[anys] * 7 + [sm] + [vm] * 6 + [sm],
        out_specs=(anys, anys, anys, vm, vm, sm),
        scratch_shapes=[
            V((toks, width), bf16), V((toks, width), bf16), V((toks, width), bf16), V((toks, width), bf16),
            V((width, ff), bf16), V((width, ff), bf16), V((ff, width), bf16),
            V((toks, ff), f32), V((toks, ff), f32), V((toks, ff), bf16),
            V((2, tb, width), f32), V((2, tb, width), f32),
            V((width, toks), bf16), V((ff, toks), bf16), V((toks, width), bf16),
            V((toks, ff), bf16), V((toks, ff), bf16),
            V((width, ff), f32), V((width, ff), f32), V((ff, width), f32),
            V((width, ff), bf16), V((width, ff), bf16), V((ff, width), bf16),
            V((tb, width), f32), V((tb, width), f32), V((tb, width), f32),
            V((8, h), f32), V((n, 8, h), f32), V((n, 8, half), f32), V((n, 8, half), f32),
            V((8, half), f32), V((2, 8, half), f32),
            V((6, 8, 256), f32), V((2, 8, 128), f32), V((2, 8, 128), f32), V((8, h), f32),
            V((8, 128), f32), V((8, 128), f32), V((8, 128), f32), V((n, 8, 128), f32),
            dma((7,)), dma((3,)), dma((n,)), dma((n,)), dma((n,)), dma((n,)), dma((n,)), dma((n,)),
            dma((6,)), dma((6,)),
        ],
        compiler_params=pltpu.CompilerParams(
            collective_id=0, has_side_effects=True, vmem_limit_bytes=62 * 1024 * 1024
        ),
    )(tokens, targets, mtokens, mtargets, gate, up, down, step, hid, cell, rw, iw, bias[None], cw, mlp)
    return (*outs[:5], outs[5][0, 0])


def solution(mesh):
    return jax.shard_map(
        local,
        mesh=mesh,
        in_specs=(
            P("task", None, None),
            P("task", None, None),
            P("task", None, None),
            P("task", None, None),
            P("task", None, "shard"),
            P("task", None, "shard"),
            P("task", "shard", None),
            P("task"),
            P("task", None, None),
            P("task", None, None),
            P("task", None),
            P(),
            P(),
            P(),
            P(),
        ),
        out_specs=(
            P("task", None, "shard"),
            P("task", None, "shard"),
            P("task", "shard", None),
            P("task", None, None),
            P("task", None, None),
            P(),
        ),
        check_vma=False,
    )
```

time: 226 us -> 84.9 us (0.38)
  Pallas kernels: 0 us -> 68.8 us
  other arithmetic: 59.9 us -> 0 us
  waiting for transfers between devices: 48.1 us -> 0 us
  blocking collectives: 43.1 us -> 0 us
  matrix products: 35.7 us -> 0 us
  between operations: 22.6 us -> 3.05 us
  local copies, waits for them, and re-layouts: 15.8 us -> 12.6 us
    pallas_call x0 -> x1, Pallas kernels: none -> 68.8 us  [local(): pl.pallas_call(functools.partial(kernel, n), out_shape=(jax.ShapeDtypeStr...]
    broadcast_in_dim x3 -> x0, other arithmetic: 48.1 us -> none  [the longest x1 16.5 us: local(): results[2][0][None]]
    psum x2 -> x0, blocking collectives: 43.1 us -> none  [the longest x1 40.5 us: local(): summed = lax.psum(meta_part, ('task', 'shard'))]
    dot_general x12 -> x0, matrix products: 35.7 us -> none  [the longest x2 10.1 us: block_forward(): output = jnp.dot(activated, w_down, preferred_element_type=jnp.float32)]
    all_gather x1 -> x0, waiting for transfers between devices: 33.4 us -> none  [local(): lax.all_gather(recurrent_weight, 'task', axis=0, tiled=True)]
    psum x1 -> x0, waiting for transfers between devices: 12 us -> none  [local(): output = lax.psum(partial_out, 'shard')]
    reduce_sum x4 -> x0, other arithmetic: 7.81 us -> none  [the longest x3 5.71 us: local(): jnp.sum(jnp.square(param_piece.astype(jnp.float32)))]
    another operation x2 -> x0, other arithmetic: 3.87 us -> none  [local(): tensor_sums = lax.psum(jnp.stack([grad_sq, param_sq]), 'shard')]
  transfers between devices with their start and end apart: 3 -> 0, of which waited for: 3 -> 0; matrix products, arithmetic and copies ran while one was open for 16% -> 0% of each run, Pallas kernels for 0% -> 0%
where the time goes in v1:
time: 84.9 us; the launch traced here: 84.5 us
  Pallas kernels  68.8 us (81%)
  local copies, waits for them, and re-layouts  12.6 us (15%)
  between operations  3.05 us (4%)
    pallas_call x1, Pallas kernels, local(): pl.pallas_call(functools.partial(kernel, n), out_shape=(jax.ShapeDtypeStr...  68.8 us
    unnamed x12, local copies, waits for them, and re-layouts  12.6 us

profile of v1, /device:TPU:0, one launch (start us, length us, event | category | flops | bytes accessed | tf_op | source)
XLA Modules:
  0.0 84.5 jit_solution(7512195515898942446)
XLA Ops:
  1.3 1.3 %copy.21.hid_ref = f32[1,3,512]{2,1,0:T(4,128)} copy(f32[1,3,512]{2,0,1:T(1,128)} %param.23) | data formatting | bytes 12288 | tf_op args[8]
  2.6 1.3 %copy.22.cell_ref = f32[1,3,512]{2,1,0:T(4,128)} copy(f32[1,3,512]{2,0,1:T(1,128)} %param.24) | data formatting | bytes 12288 | tf_op args[9]
  3.9 1.6 %copy.23.cw_ref = f32[512,5]{1,0:T(8,128)} copy(f32[512,5]{0,1:T(8,128)} %param.28) | data formatting | bytes 20480 | tf_op args[13]
  5.4 68.8 %shard_map.190 = (bf16[1,1024,768]{2,1,0:T(8,128)(2,1)}, bf16[1,1024,768]{2,1,0:T(8,128)(2,1)}, bf16[1,768,1024]{2,1,0:T(8,128)(2,1)}, f32[1,3,512]{2,1,0:T(4,12...) custom-call(bf16[1,512,1024]{2,1,0:T(8,128)(2,1)} %tok_hbm.1, bf16[1,512,1024]{2,1,0:T(8,128)(2,1)} %tgt_hbm.1, ...), custom_call_target="tpu_custom_call" | custom-call | tf_op jit(solution)/shard_map/pallas_call | solution.py:311
  74.3 1.3 %copy.24 = f32[1,3,512]{2,0,1:T(1,128)} copy(f32[1,3,512]{2,1,0:T(4,128)} %get-tuple-element.21) | data formatting | bytes 12288
  75.6 1.3 %copy.25 = f32[1,3,512]{2,0,1:T(1,128)} copy(f32[1,3,512]{2,1,0:T(4,128)} %get-tuple-element.22) | data formatting | bytes 12288
  76.9 0.0 copy-start.1
  76.9 2.8 %copy.31 = bf16[1,1024,768]{2,1,0:T(8,128)(2,1)} copy(bf16[1,1024,768]{2,1,0:T(8,128)(2,1)} %get-tuple-element.30) | data formatting | bytes 3145728
  79.6 0.0 copy-done.1
  79.6 0.0 copy-start
  79.6 1.1 %copy.32 = bf16[1,1024,768]{2,1,0:T(8,128)(2,1)} copy(bf16[1,1024,768]{2,1,0:T(8,128)(2,1)S(1)} %copy-done.1) | data formatting | bytes 3145728
  80.8 0.8 copy-done
  81.6 1.1 %copy.33 = bf16[1,768,1024]{2,1,0:T(8,128)(2,1)} copy(bf16[1,768,1024]{2,1,0:T(8,128)(2,1)S(1)} %copy-done) | data formatting | bytes 3145728
Async XLA Ops:
  76.9 2.8 %copy-start.1 = (bf16[1,1024,768]{2,1,0:T(8,128)(2,1)S(1)}, bf16[1,1024,768]{2,1,0:T(8,128)(2,1)}, u32[]{:S(2)}) copy-start(bf16[1,1024,768]{2,1,0:T(8,128)(2,1)} %get-tuple-element.31) | copy-start | bytes 4718596
  79.6 2.0 %copy-start = (bf16[1,768,1024]{2,1,0:T(8,128)(2,1)S(1)}, bf16[1,768,1024]{2,1,0:T(8,128)(2,1)}, u32[]{:S(2)}) copy-start(bf16[1,768,1024]{2,1,0:T(8,128)(2,1)} %get-tuple-element.32) | copy-start | bytes 4718596

commit v2 on v1

--- a/solution.py
+++ b/solution.py
@@ -74,9 +74,11 @@
         c.start()
 
     hid_pad[...] = jnp.zeros_like(hid_pad)
-    hid_pad[0:3, :] = hid_ref[0]
+    for t in range(3):
+        hid_pad[t:t + 1, :] = hid_ref[t]
     cell_pad[...] = jnp.zeros_like(cell_pad)
-    cell_pad[0:3, :] = cell_ref[0]
+    for t in range(3):
+        cell_pad[t:t + 1, :] = cell_ref[t]
     sq[...] = jnp.zeros_like(sq)
     hid_all[me] = hid_pad[...]
 
@@ -102,7 +104,7 @@
     ins[1].wait()
     ins[2].wait()
 
-    def hidden(x, w1, w2, keep):
+    def hidden(x, w1, w2, keep, beside=None):
         @pl.loop(0, ff // fbk)
         def _(j):
             fs = pl.ds(pl.multiple_of(j * fbk, fbk), fbk)
@@ -116,6 +118,8 @@
                 if keep:
                     fa[ts, fs] = a
                     fb[ts, fs] = u * s * (1.0 + g * (1.0 - s))
+                if beside is not None:
+                    beside(2 * j + i, fbk // 2)
 
     hidden(tok, gate, up, True)
     ins[3].wait()
@@ -201,7 +205,7 @@
     rec_full[core] = rec_half[...]
 
     to_sib(stat, stat_recv, 2).wait()
-    entries = 2.0 * (width * ff)
+    entries = float(width * ff * lax.axis_size("shard"))
     rms = jnp.sqrt((stat[...] + stat_recv[...]) / entries + epsilon)
     rms_g, rms_p = rms[0], rms[1]
     lg, lp = jnp.log(rms_g)[:, 0:1], jnp.log(rms_p)[:, 0:1]
@@ -218,43 +222,55 @@
 
     cell = jax.nn.sigmoid(block(1)) * cell_pad[...] + jax.nn.sigmoid(block(0)) * jnp.tanh(block(2))
     hid = jax.nn.sigmoid(block(3)) * jnp.tanh(cell)
-    nc_ref[0] = cell[0:3]
-    nh_ref[0] = hid[0:3]
-    ctx = dot(hid, cw_ref[...], precision=highest)
+    for t in range(3):
+        nc_ref[t] = cell[t:t + 1]
+        nh_ref[t] = hid[t:t + 1]
+    ctx = dot(hid, cw_ref[...], ((1,), (1,)), precision=highest)
 
     units = mlp_ref.shape[1]
 
-    def update(t, w, g, out, out_hbm):
+    def coefs(t):
         rp, rg = rms_p[t:t + 1, 0:1], rms_g[t:t + 1, 0:1]
         ca = [mlp_ref[0, k] / rp for k in range(units)]
         cb = [mlp_ref[1, k] / rg for k in range(units)]
         cc = [ctx[t:t + 1, k:k + 1] for k in range(units)]
-        size = jnp.exp(ctx[t:t + 1, units:units + 1])
-        back = rate_factor * rp
-
-        @pl.loop(0, w.shape[0] // 16)
+        return ca, cb, cc, jnp.exp(ctx[t:t + 1, units:units + 1]), rate_factor * rp
+
+    def update(co, w, g, out, first, count):
+        ca, cb, cc, size, back = co
+        for i in range(count // 16):
+            rows = pl.ds(pl.multiple_of(first + i * 16, 16), 16)
+            for q in range(w.shape[1] // 256):
+                qs = pl.ds(q * 256, 256)
+                p = w[rows, qs].astype(f32)
+                gv = g[rows, qs]
+                acc = None
+                for k in range(units):
+                    term = mlp_ref[2, k] * jnp.maximum(ca[k] * p + cb[k] * gv + cc[k], 0.0)
+                    acc = term if acc is None else acc + term
+                upd = size * acc
+                out[rows, qs] = upd.astype(bf16)
+                w[rows, qs] = (p - back * upd).astype(bf16)
+
+    outs = []
+    for t, (w, g, o, oh) in enumerate(((gate, gg, ug, gu_hbm), (up, gu, uu, uu_hbm))):
+        co = coefs(t)
+
+        @pl.loop(0, w.shape[0] // 32)
         def _(i):
-            rows = pl.ds(pl.multiple_of(i * 16, 16), 16)
-            p = w[rows, :].astype(f32)
-            gv = g[rows, :]
-            acc = None
-            for k in range(units):
-                term = mlp_ref[2, k] * jnp.maximum(ca[k] * p + cb[k] * gv + cc[k], 0.0)
-                acc = term if acc is None else acc + term
-            upd = size * acc
-            out[rows, :] = upd.astype(bf16)
-            w[rows, :] = (p - back * upd).astype(bf16)
-
-        return pltpu.make_async_copy(out, out_hbm.at[0], out_sem.at[t])
-
-    outs = []
-    for t, (w, g, o, oh) in enumerate(((gate, gg, ug, gu_hbm), (up, gu, uu, uu_hbm), (down, gd, ud, du_hbm))):
-        c = update(t, w, g, o, oh)
+            update(co, w, g, o, i * 32, 32)
+
+        c = pltpu.make_async_copy(o, oh.at[0], out_sem.at[t])
         c.start()
         outs.append(c)
 
+    co = coefs(2)
+
     ins[5].wait()
-    hidden(mtok, gate, up, False)
+    hidden(mtok, gate, up, False, lambda i, c: update(co, down, gd, ud, i * c, c))
+    c = pltpu.make_async_copy(ud, du_hbm.at[0], out_sem.at[2])
+    c.start()
+    outs.append(c)
     msend[...] = dot(act[pl.ds(pl.multiple_of(sib * tb, tb), tb), :], down[...])
     to_sib(msend, mrecv, 4).start()
     own = pl.multiple_of(core * tb, tb)
@@ -314,11 +330,11 @@
             jax.ShapeDtypeStruct(gate.shape, bf16),
             jax.ShapeDtypeStruct(up.shape, bf16),
             jax.ShapeDtypeStruct(down.shape, bf16),
-            jax.ShapeDtypeStruct(hid.shape, f32),
-            jax.ShapeDtypeStruct(cell.shape, f32),
+            jax.ShapeDtypeStruct((hid.shape[1], 1, h), f32),
+            jax.ShapeDtypeStruct((hid.shape[1], 1, h), f32),
             jax.ShapeDtypeStruct((1, 1), f32),
         ),
-        in_specs=[anys] * 7 + [sm] + [vm] * 6 + [sm],
+        in_specs=[pl.BlockSpec(memory_space=pltpu.HBM)] * 7 + [sm] + [vm] * 6 + [sm],
         out_specs=(anys, anys, anys, vm, vm, sm),
         scratch_shapes=[
             V((toks, width), bf16), V((toks, width), bf16), V((toks, width), bf16), V((toks, width), bf16),
@@ -338,10 +354,10 @@
             dma((6,)), dma((6,)),
         ],
         compiler_params=pltpu.CompilerParams(
-            collective_id=0, has_side_effects=True, vmem_limit_bytes=62 * 1024 * 1024
+            collective_id=0, has_side_effects=True, vmem_limit_bytes=58 * 1024 * 1024
         ),
-    )(tokens, targets, mtokens, mtargets, gate, up, down, step, hid, cell, rw, iw, bias[None], cw, mlp)
-    return (*outs[:5], outs[5][0, 0])
+    )(tokens, targets, mtokens, mtargets, gate, up, down, step, jnp.swapaxes(hid, 0, 1), jnp.swapaxes(cell, 0, 1), rw, iw, bias[None], cw.T, mlp)
+    return (*outs[:3], jnp.swapaxes(outs[3], 0, 1), jnp.swapaxes(outs[4], 0, 1), outs[5][0, 0])
 
 
 def solution(mesh):

time: 84.9 us -> 69.3 us (0.82)
  Pallas kernels: 68.8 us -> 59 us
  local copies, waits for them, and re-layouts: 12.6 us -> 7.08 us
    pallas_call x1, Pallas kernels: 68.8 us -> 59 us  [local(): pl.pallas_call(functools.partial(kernel, n), out_shape=(jax.ShapeDtypeStr...]
    unnamed x12 -> x13, local copies, waits for them, and re-layouts: 12.6 us -> 7.08 us
where the time goes in v2:
time: 69.3 us; the launch traced here: 69.1 us
  Pallas kernels  59 us (85%)
  local copies, waits for them, and re-layouts  7.08 us (10%)
  between operations  3.07 us (4%)
    pallas_call x1, Pallas kernels, local(): pl.pallas_call(functools.partial(kernel, n), out_shape=(jax.ShapeDtypeStr...  59 us
    unnamed x13, local copies, waits for them, and re-layouts  7.08 us

profile of v2, /device:TPU:0, one launch (start us, length us, event | category | flops | bytes accessed | tf_op | source)
XLA Modules:
  0.0 69.1 jit_solution(18104690751768284065)
XLA Ops:
  1.3 59.0 %shard_map.190 = (bf16[1,1024,768]{2,1,0:T(8,128)(2,1)}, bf16[1,1024,768]{2,1,0:T(8,128)(2,1)}, bf16[1,768,1024]{2,1,0:T(8,128)(2,1)}, f32[3,1,512]{2,1,0:T(1,12...) custom-call(bf16[1,512,1024]{2,1,0:T(8,128)(2,1)} %tok_hbm.1, bf16[1,512,1024]{2,1,0:T(8,128)(2,1)} %tgt_hbm.1, ...), custom_call_target="tpu_custom_call" | custom-call | tf_op jit(solution)/shard_map/pallas_call | solution.py:327
  60.2 0.0 copy-start.1
  60.3 2.8 %copy.28 = bf16[1,1024,768]{2,1,0:T(8,128)(2,1)} copy(bf16[1,1024,768]{2,1,0:T(8,128)(2,1)} %get-tuple-element.24) | data formatting | bytes 3145728
  63.0 0.0 copy-done.1
  63.0 0.0 copy-start
  63.0 1.1 %copy.29 = bf16[1,1024,768]{2,1,0:T(8,128)(2,1)} copy(bf16[1,1024,768]{2,1,0:T(8,128)(2,1)S(1)} %copy-done.1) | data formatting | bytes 3145728
  64.2 0.8 %copy-done = bf16[1,768,1024]{2,1,0:T(8,128)(2,1)S(1)} copy-done((bf16[1,768,1024]{2,1,0:T(8,128)(2,1)S(1)}, bf16[1,768,1024]{2,1,0:T(8,128)(2,1)}, u32[]{:S(2)}) %copy-start) | copy-done | bytes 1572888
  65.0 0.0 copy-start.3
  65.0 0.0 copy-start.2
  65.0 1.1 %copy.30 = bf16[1,768,1024]{2,1,0:T(8,128)(2,1)} copy(bf16[1,768,1024]{2,1,0:T(8,128)(2,1)S(1)} %copy-done) | data formatting | bytes 3145728
  66.2 0.0 copy-done.3
  66.2 0.6 copy.31
  66.7 0.0 copy-done.2
  66.8 0.6 copy.32
Async XLA Ops:
  60.2 2.8 %copy-start.1 = (bf16[1,1024,768]{2,1,0:T(8,128)(2,1)S(1)}, bf16[1,1024,768]{2,1,0:T(8,128)(2,1)}, u32[]{:S(2)}) copy-start(bf16[1,1024,768]{2,1,0:T(8,128)(2,1)} %get-tuple-element.25) | copy-start | bytes 4718596
  63.0 2.0 %copy-start = (bf16[1,768,1024]{2,1,0:T(8,128)(2,1)S(1)}, bf16[1,768,1024]{2,1,0:T(8,128)(2,1)}, u32[]{:S(2)}) copy-start(bf16[1,768,1024]{2,1,0:T(8,128)(2,1)} %get-tuple-element.26) | copy-start | bytes 4718596
  65.0 1.1 %copy-start.3 = (f32[3,1,512]{2,1,0:T(1,128)S(1)}, f32[3,1,512]{2,1,0:T(1,128)}, u32[]{:S(2)}) copy-start(f32[3,1,512]{2,1,0:T(1,128)} %get-tuple-element.15) | copy-start | bytes 18436
  65.0 1.7 %copy-start.2 = (f32[3,1,512]{2,1,0:T(1,128)S(1)}, f32[3,1,512]{2,1,0:T(1,128)}, u32[]{:S(2)}) copy-start(f32[3,1,512]{2,1,0:T(1,128)} %get-tuple-element.16) | copy-start | bytes 18436

commit v3 on v2

--- a/solution.py
+++ b/solution.py
@@ -234,7 +234,9 @@
         ca = [mlp_ref[0, k] / rp for k in range(units)]
         cb = [mlp_ref[1, k] / rg for k in range(units)]
         cc = [ctx[t:t + 1, k:k + 1] for k in range(units)]
-        return ca, cb, cc, jnp.exp(ctx[t:t + 1, units:units + 1]), rate_factor * rp
+        size = jnp.exp(ctx[t:t + 1, units:units + 1])
+        one = lambda x: x[0, 0]
+        return [one(x) for x in ca], [one(x) for x in cb], [one(x) for x in cc], one(size), one(rate_factor * rp)
 
     def update(co, w, g, out, first, count):
         ca, cb, cc, size, back = co
@@ -256,9 +258,9 @@
     for t, (w, g, o, oh) in enumerate(((gate, gg, ug, gu_hbm), (up, gu, uu, uu_hbm))):
         co = coefs(t)
 
-        @pl.loop(0, w.shape[0] // 32)
+        @pl.loop(0, w.shape[0] // 64)
         def _(i):
-            update(co, w, g, o, i * 32, 32)
+            update(co, w, g, o, i * 64, 64)
 
         c = pltpu.make_async_copy(o, oh.at[0], out_sem.at[t])
         c.start()

time: 69.3 us -> 64.6 us (0.932)
  Pallas kernels: 59 us -> 54.3 us
    pallas_call x1, Pallas kernels: 59 us -> 54.3 us  [local(): pl.pallas_call(functools.partial(kernel, n), out_shape=(jax.ShapeDtypeStr...]
where the time goes in v3:
time: 64.6 us; the launch traced here: 64.5 us
  Pallas kernels  54.3 us (84%)
  local copies, waits for them, and re-layouts  7.08 us (11%)
  between operations  3.07 us (5%)
    pallas_call x1, Pallas kernels, local(): pl.pallas_call(functools.partial(kernel, n), out_shape=(jax.ShapeDtypeStr...  54.3 us
    unnamed x13, local copies, waits for them, and re-layouts  7.08 us

profile of v3, /device:TPU:0, one launch (start us, length us, event | category | flops | bytes accessed | tf_op | source)
XLA Modules:
  0.0 64.5 jit_solution(9056205174244235097)
XLA Ops:
  1.3 54.3 %shard_map.190 = (bf16[1,1024,768]{2,1,0:T(8,128)(2,1)}, bf16[1,1024,768]{2,1,0:T(8,128)(2,1)}, bf16[1,768,1024]{2,1,0:T(8,128)(2,1)}, f32[3,1,512]{2,1,0:T(1,12...) custom-call(bf16[1,512,1024]{2,1,0:T(8,128)(2,1)} %tok_hbm.1, bf16[1,512,1024]{2,1,0:T(8,128)(2,1)} %tgt_hbm.1, ...), custom_call_target="tpu_custom_call" | custom-call | tf_op jit(solution)/shard_map/pallas_call | solution.py:329
  55.6 0.0 copy-start.1
  55.6 2.8 %copy.28 = bf16[1,1024,768]{2,1,0:T(8,128)(2,1)} copy(bf16[1,1024,768]{2,1,0:T(8,128)(2,1)} %get-tuple-element.24) | data formatting | bytes 3145728
  58.4 0.0 copy-done.1
  58.4 0.0 copy-start
  58.4 1.1 %copy.29 = bf16[1,1024,768]{2,1,0:T(8,128)(2,1)} copy(bf16[1,1024,768]{2,1,0:T(8,128)(2,1)S(1)} %copy-done.1) | data formatting | bytes 3145728
  59.5 0.8 %copy-done = bf16[1,768,1024]{2,1,0:T(8,128)(2,1)S(1)} copy-done((bf16[1,768,1024]{2,1,0:T(8,128)(2,1)S(1)}, bf16[1,768,1024]{2,1,0:T(8,128)(2,1)}, u32[]{:S(2)}) %copy-start) | copy-done | bytes 1572888
  60.3 0.0 copy-start.3
  60.4 0.0 copy-start.2
  60.4 1.1 %copy.30 = bf16[1,768,1024]{2,1,0:T(8,128)(2,1)} copy(bf16[1,768,1024]{2,1,0:T(8,128)(2,1)S(1)} %copy-done) | data formatting | bytes 3145728
  61.5 0.0 copy-done.3
  61.5 0.6 copy.31
  62.1 0.0 copy-done.2
  62.1 0.6 copy.32
Async XLA Ops:
  55.6 2.8 %copy-start.1 = (bf16[1,1024,768]{2,1,0:T(8,128)(2,1)S(1)}, bf16[1,1024,768]{2,1,0:T(8,128)(2,1)}, u32[]{:S(2)}) copy-start(bf16[1,1024,768]{2,1,0:T(8,128)(2,1)} %get-tuple-element.25) | copy-start | bytes 4718596
  58.4 2.0 %copy-start = (bf16[1,768,1024]{2,1,0:T(8,128)(2,1)S(1)}, bf16[1,768,1024]{2,1,0:T(8,128)(2,1)}, u32[]{:S(2)}) copy-start(bf16[1,768,1024]{2,1,0:T(8,128)(2,1)} %get-tuple-element.26) | copy-start | bytes 4718596
  60.3 1.1 %copy-start.3 = (f32[3,1,512]{2,1,0:T(1,128)S(1)}, f32[3,1,512]{2,1,0:T(1,128)}, u32[]{:S(2)}) copy-start(f32[3,1,512]{2,1,0:T(1,128)} %get-tuple-element.15) | copy-start | bytes 18436
  60.4 1.7 %copy-start.2 = (f32[3,1,512]{2,1,0:T(1,128)S(1)}, f32[3,1,512]{2,1,0:T(1,128)}, u32[]{:S(2)}) copy-start(f32[3,1,512]{2,1,0:T(1,128)} %get-tuple-element.16) | copy-start | bytes 18436

commit v4 on v3

--- a/solution.py
+++ b/solution.py
@@ -310,6 +310,26 @@
         to_task(loss_chip, loss_all, loss_s, loss_r, s, s).wait_recv()
 
     loss_ref[0, 0] = jnp.sum(jnp.sum(loss_all[...], axis=0)) * (0.5 / (toks * width)) / n
+
+
+def hand_out(count, *refs):
+    srcs, dsts, bufs = refs[:count], refs[count:2 * count], refs[2 * count:3 * count]
+    in_sem, out_sem = refs[3 * count:]
+    loads, stores = [], []
+    for i in range(count):
+        rows = bufs[i].shape[0]
+        parts = 2 if rows % 32 == 0 else 1
+        for q in range(parts):
+            rs = pl.ds(q * (rows // parts), rows // parts)
+            loads.append(pltpu.make_async_copy(srcs[i].at[rs], bufs[i].at[rs], in_sem.at[2 * i + q]))
+            stores.append(pltpu.make_async_copy(bufs[i].at[rs], dsts[i].at[rs], out_sem.at[2 * i + q]))
+    for c in loads:
+        c.start()
+    for c, d in zip(loads, stores):
+        c.wait()
+        d.start()
+    for d in stores:
+        d.wait()
 
 
 def local(*args):
@@ -359,6 +379,16 @@
             collective_id=0, has_side_effects=True, vmem_limit_bytes=58 * 1024 * 1024
         ),
     )(tokens, targets, mtokens, mtargets, gate, up, down, step, jnp.swapaxes(hid, 0, 1), jnp.swapaxes(cell, 0, 1), rw, iw, bias[None], cw.T, mlp)
+    sent = [x[0] for x in outs[:3]] + list(outs[3:5])
+    moved = pl.pallas_call(
+        functools.partial(hand_out, len(sent)),
+        out_shape=tuple(jax.ShapeDtypeStruct(x.shape, x.dtype) for x in sent),
+        in_specs=[anys] * len(sent),
+        out_specs=(anys,) * len(sent),
+        scratch_shapes=[V(x.shape, x.dtype) for x in sent] + [dma((2 * len(sent),)), dma((2 * len(sent),))],
+        compiler_params=pltpu.CompilerParams(vmem_limit_bytes=58 * 1024 * 1024),
+    )(*sent)
+    outs = [x[None] for x in moved[:3]] + list(moved[3:]) + [outs[5]]
     return (*outs[:3], jnp.swapaxes(outs[3], 0, 1), jnp.swapaxes(outs[4], 0, 1), outs[5][0, 0])
 
 

time: 64.6 us -> 61.6 us (0.954)
  local copies, waits for them, and re-layouts: 7.08 us -> 0 us
  Pallas kernels: 54.3 us -> 58.3 us
    unnamed x13 -> x0, local copies, waits for them, and re-layouts: 7.08 us -> none
    pallas_call x0 -> x1, Pallas kernels: none -> 4.04 us  [local(): pl.pallas_call(functools.partial(hand_out, len(sent)), out_shape=tuple((j...]
where the time goes in v4:
time: 61.6 us; the launch traced here: 61.4 us
  Pallas kernels  58.3 us (95%)
  between operations  3.05 us (5%)
    pallas_call x1, Pallas kernels, local(): pl.pallas_call(functools.partial(kernel, n), out_shape=(jax.ShapeDtypeStr...  54.3 us
    pallas_call x1, Pallas kernels, local(): pl.pallas_call(functools.partial(hand_out, len(sent)), out_shape=tuple((j...  4.04 us

profile of v4, /device:TPU:0, one launch (start us, length us, event | category | flops | bytes accessed | tf_op | source)
XLA Modules:
  0.0 61.4 jit_solution(16773697428056804604)
XLA Ops:
  1.3 54.3 %shard_map.190 = (bf16[1,1024,768]{2,1,0:T(8,128)(2,1)}, bf16[1,1024,768]{2,1,0:T(8,128)(2,1)}, bf16[1,768,1024]{2,1,0:T(8,128)(2,1)}, f32[3,1,512]{2,1,0:T(1,12...) custom-call(bf16[1,512,1024]{2,1,0:T(8,128)(2,1)} %tok_hbm.1, bf16[1,512,1024]{2,1,0:T(8,128)(2,1)} %tgt_hbm.1, ...), custom_call_target="tpu_custom_call" | custom-call | tf_op jit(solution)/shard_map/pallas_call | solution.py:349
  55.6 4.0 %shard_map.191 = (bf16[1024,768]{1,0:T(8,128)(2,1)}, bf16[1024,768]{1,0:T(8,128)(2,1)}, bf16[768,1024]{1,0:T(8,128)(2,1)}, f32[3,1,512]{2,1,0:T(1,128)}, f32[3,1,512]{2,1,0:T(1,128)}) custom-call(bf16[1024,768]{1,0:T(8,128)(2,1)} %bitcast.13, bf16[1024,768]{1,0:T(8,128)(2,1)} %bitcast.14, bf16[768,1024]{1,0:T(8,128)(2,1)} %bitcast.15, ...), custom_call_target="tpu_custom_call" | custom-call | tf_op jit(solution)/shard_map/pallas_call | solution.py:383
